TPU v7x, 256 devices: a whole 4x4x8 slice. The times are simulated.
256 devices in a mesh: tm: 16 (over x, y), space: 16 (over z, core).
Axes of the slice: x: 4, y: 4, z: 8, core: 2. Of those that a mesh axis runs over, the one named last changes fastest.
Arguments:
- snapshots: bfloat16 [16, 128, 4, 32, 16, 256], P('tm', None, None, 'space'), may hold values from -8 to 8, as said below
- lat_taps: float32 [4, 32, 5], P(None, 'space'), may hold values from 0.1 to 1
- lon_taps: float32 [4, 32, 5], P(None, 'space'), may hold values from 0.1 to 1
Outputs:
- merged: bfloat16 [16, 128, 4, 32, 1024], P('tm', None, None, 'space')
Inputs may be any that keep to these rules, and one draw needn't show every extreme that they name: `snapshots`: Real-valued hourly fields of the window.
All inputs are finite; a program needn't handle non-finite values.
Results may differ from a plain program's by a relative error of at most 0.025.
Values may be sent and summed in bfloat16 or wider, within the bound.
A program may use at most 128 MiB of HBM per device.

v0:
```python
import math

import jax
import jax.numpy as jnp
from jax import lax
from jax.sharding import PartitionSpec as P

RANK = 128
LEVEL = 0
ITERS = 4


def from_partner(value, axis, distance):
    mask = 2**distance
    pairs = [(source, source ^ mask) for source in range(lax.axis_size(axis))]
    return lax.ppermute(value, axis, pairs)


def band_matrix(filter_weights, fine_len, coarse_len):
    reach = filter_weights.shape[-1] // 2
    fine_index = jnp.arange(fine_len)[:, None]
    coarsened_grid_index = jnp.arange(coarse_len)[None, :]
    offset = fine_index - 2 * coarsened_grid_index + reach
    indicator_vector = (
        offset[:, :, None] == jnp.arange(filter_weights.shape[-1])[None, None, :]
    ).astype(jnp.float32)
    return jnp.einsum(
        "pyu,shu->pysh", filter_weights, indicator_vector, precision=lax.Precision.HIGHEST
    )


def split_pair(singular_values):
    high_part = singular_values.astype(jnp.bfloat16)
    low_part = (singular_values - high_part.astype(jnp.float32)).astype(jnp.bfloat16)
    return (high_part, low_part)


def coarsen(fine_field, lat_taps, lon_taps):
    fine_rows = fine_field.shape[-2]
    fine_cols = fine_field.shape[-1]
    lon_matrix = band_matrix(lon_taps, fine_cols, fine_cols // 2)
    lon_high, lon_low = split_pair(lon_matrix)
    across = jnp.einsum(
        "svlrf,vlfc->svlrc", fine_field, lon_high, preferred_element_type=jnp.float32
    )
    across = across + jnp.einsum(
        "svlrf,vlfc->svlrc", fine_field, lon_low, preferred_element_type=jnp.float32
    )
    lat_matrix = band_matrix(lat_taps, fine_rows, fine_rows // 2)
    result = jnp.einsum("svlrc,vlri->svlic", across, lat_matrix, precision=lax.Precision.HIGHEST)
    shape_head = fine_field.shape[:3]
    return result.astype(jnp.bfloat16).reshape(shape_head + (fine_rows // 2 * (fine_cols // 2),))


def orthonormal(image_cols):
    product = jnp.dot(image_cols.T, image_cols, precision=lax.Precision.HIGHEST)
    factor = jnp.linalg.cholesky(product)
    return jax.scipy.linalg.solve_triangular(factor, image_cols.T, lower=True).T


def local(snapshots, lat_taps, lon_taps):
    coarse = coarsen(snapshots[0], lat_taps, lon_taps)
    snap_count, variable_total, level_count, cell_count = coarse.shape
    row_count = variable_total * level_count * cell_count
    own_block = coarse.reshape(snap_count, row_count)
    upper_bit = lax.axis_index("tm") // 2**LEVEL % 2
    lower_block_leading = upper_bit == 0
    partner = from_partner(own_block, "tm", LEVEL)
    stacked = jnp.concatenate(
        [
            jnp.where(lower_block_leading, own_block, partner),
            jnp.where(lower_block_leading, partner, own_block),
        ],
        axis=0,
    )
    initial = (jnp.arange(2 * snap_count)[:, None] % RANK == jnp.arange(RANK)[None, :]).astype(
        jnp.float32
    )
    basis_cols = initial
    for sweep in range(ITERS):
        basis_high, basis_low = split_pair(basis_cols)
        projected = lax.dot_general(
            basis_high, stacked, (((0,), (0,)), ((), ())), preferred_element_type=jnp.float32
        )
        projected = projected + lax.dot_general(
            basis_low, stacked, (((0,), (0,)), ((), ())), preferred_element_type=jnp.float32
        )
        proj_high, proj_low = split_pair(projected)
        image_cols = lax.dot_general(
            stacked, proj_high, (((1,), (1,)), ((), ())), preferred_element_type=jnp.float32
        )
        image_cols = image_cols + lax.dot_general(
            stacked, proj_low, (((1,), (1,)), ((), ())), preferred_element_type=jnp.float32
        )
        image_cols = lax.psum(image_cols, "space")
        basis_cols = orthonormal(image_cols)
    coefficients = basis_cols.astype(jnp.bfloat16)
    product = lax.dot_general(
        coefficients, stacked, (((0,), (0,)), ((), ())), preferred_element_type=jnp.float32
    )
    merged_rows = (product * (1.0 / math.sqrt(2 * snap_count))).astype(jnp.bfloat16)
    return merged_rows.reshape(1, RANK, variable_total, level_count, cell_count)


def solution(mesh):
    in_specs = (
        P("tm", None, None, "space", None, None),
        P(None, "space", None),
        P(None, "space", None),
    )
    out_specs = P("tm", None, None, "space", None)
    return jax.shard_map(local, mesh=mesh, in_specs=in_specs, out_specs=out_specs, check_vma=False)
```

profile of v0, /device:TPU:1, one launch (start us, length us, event | category | flops | bytes accessed | tf_op | source)
XLA Modules:
  0.0 679.0 jit_solution(5254708278556308869)
XLA Ops:
  6.6 1.9 fusion.24
  8.5 9.1 %fusion.4 = f32[4,2,128,128,16]{2,4,3,1,0:T(8,128)} fusion(bf16[4,2,256,128,1]{3,0,1,2,4:T(4,128)(2,1)S(1)} %get-tuple-element.9, bf16[1,128,4,2,16,256]{5,4,3,2,1,0:T(8,128)(2,1)} %param.6), kind=kOutput, calls=%fused_computation.9 | convolution fusion | flops 1073741824 | bytes 17301504 | tf_op jit(solution)/shard_map/svlrf,vlfc->svlrc/dot_general | solution.py:46
  17.6 5.6 fusion.6
  23.9 8.1 %convert_bitcast_fusion = bf16[128,4,2,8,128]{4,3,0,2,1:T(8,128)(2,1)S(1)} fusion(f32[4,2,128,128,16]{2,4,3,1,0:T(8,128)} %fusion.6, f32[4,2,128,128,16]{2,4,3,1,0:T(8,128)} %fusion.4, f32[16,8,4,2]{0,1,3,2:T(8,128)S(1)} %copy.17), kind=kOutput, calls=%fused_computation.22 | convolution fusion | flops 204472320 | bytes 18878464 | tf_op jit(solution)/shard_map/svlrc,vlri->svlic/dot_general | solution.py:50
  32.0 2.6 copy.10
  34.6 2.3 collective-permute-start
  36.9 44.5 %collective-permute-done = bf16[128,8192]{0,1:T(8,128)(2,1)} collective-permute-done((bf16[128,8192]{0,1:T(8,128)(2,1)}, bf16[128,8192]{0,1:T(8,128)(2,1)}, u32[]{:S(2)}, u32[]{:S(2)}) %collective-permute-start) | collective-permute-done | bytes 2097184 | tf_op jit(solution)/shard_map/ppermute | solution.py:16
  81.4 2.5 broadcast_select_fusion.1
  83.9 1.6 fusion.40
  85.5 1.7 convolution_add_fusion.3
  88.6 2.0 convolution_add_fusion.7
  90.6 114.7 %all-reduce.5.cloned.1.call-done = f32[256,128]{1,0:T(8,128)} async-done(((f32[256,128]{1,0:T(8,128)}), f32[256,128]{1,0:T(8,128)}) %all-reduce.5.cloned.1.call-update) | async-done | bytes 131088 | tf_op jit(solution)/shard_map/psum | solution.py:95
  206.9 11.7 %cholesky.74 = f32[128,128]{1,0:T(8,128)S(1)} custom-call(f32[128,128]{1,0:T(8,128)S(1)} %fusion.49), custom_call_target="Cholesky" | custom-call | tf_op jit(solution)/shard_map/jit(cholesky)/cholesky | solution.py:57
  219.8 9.8 %custom-call.8 = f32[1,128,128]{1,2,0:T(8,128)S(1)} custom-call(f32[1,128,128]{2,1,0:T(8,128)S(1)} %fusion.33), custom_call_target="InvertDiagBlocksLowerTriangular" | custom-call | tf_op jit(solution)/shard_map/jit(_solve_triangular)/triangular_solve | solution.py:58
  230.9 3.2 fusion.37
  237.0 2.0 convolution_add_fusion.6
  239.1 8.2 %all-reduce.9.cloned.1.call-start = ((), (), s32[]{:S(2)}) async-start(), calls=%async_computation.2 | async-start | bytes 262144 | tf_op jit(solution)/shard_map/psum | solution.py:95
  247.3 101.9 %all-reduce.7.cloned.1.call-done = f32[256,128]{1,0:T(8,128)} async-done(((f32[256,128]{1,0:T(8,128)}), f32[256,128]{1,0:T(8,128)}) %all-reduce.7.cloned.1.call-update) | async-done | bytes 131088 | tf_op jit(solution)/shard_map/psum | solution.py:95
  350.7 11.7 %cholesky.85 = f32[128,128]{1,0:T(8,128)S(1)} custom-call(f32[128,128]{1,0:T(8,128)S(1)} %fusion.47), custom_call_target="Cholesky" | custom-call | tf_op jit(solution)/shard_map/jit(cholesky)/cholesky | solution.py:57
  363.7 9.8 %custom-call.9 = f32[1,128,128]{1,2,0:T(8,128)S(1)} custom-call(f32[1,128,128]{2,1,0:T(8,128)S(1)} %fusion.34), custom_call_target="InvertDiagBlocksLowerTriangular" | custom-call | tf_op jit(solution)/shard_map/jit(_solve_triangular)/triangular_solve | solution.py:58
  374.7 3.2 fusion.38
  380.9 2.0 convolution_add_fusion.5
  383.2 110.1 %all-reduce.9.cloned.1.call-done = f32[256,128]{1,0:T(8,128)} async-done(((f32[256,128]{1,0:T(8,128)}), f32[256,128]{1,0:T(8,128)}) %all-reduce.9.cloned.1.call-update) | async-done | bytes 131088 | tf_op jit(solution)/shard_map/psum | solution.py:95
  494.8 11.7 %cholesky.96 = f32[128,128]{1,0:T(8,128)S(1)} custom-call(f32[128,128]{1,0:T(8,128)S(1)} %fusion.45), custom_call_target="Cholesky" | custom-call | tf_op jit(solution)/shard_map/jit(cholesky)/cholesky | solution.py:57
  507.7 9.8 %custom-call.10 = f32[1,128,128]{1,2,0:T(8,128)S(1)} custom-call(f32[1,128,128]{2,1,0:T(8,128)S(1)} %fusion.35), custom_call_target="InvertDiagBlocksLowerTriangular" | custom-call | tf_op jit(solution)/shard_map/jit(_solve_triangular)/triangular_solve | solution.py:58
  518.8 3.2 fusion.39
  524.9 2.0 convolution_add_fusion.4
  527.0 110.4 %all-reduce.11.cloned.1.call-done = f32[256,128]{1,0:T(8,128)} async-done(((f32[256,128]{1,0:T(8,128)}), f32[256,128]{1,0:T(8,128)}) %all-reduce.11.cloned.1.call-update) | async-done | bytes 131088 | tf_op jit(solution)/shard_map/psum | solution.py:95
  638.8 11.9 %cholesky.107 = f32[128,128]{1,0:T(8,128)S(1)} custom-call(f32[128,128]{1,0:T(8,128)S(1)} %fusion.43), custom_call_target="Cholesky" | custom-call | tf_op jit(solution)/shard_map/jit(cholesky)/cholesky | solution.py:57
  652.0 9.8 %custom-call.11 = f32[1,128,128]{1,2,0:T(8,128)S(1)} custom-call(f32[1,128,128]{2,1,0:T(8,128)S(1)} %fusion.36), custom_call_target="InvertDiagBlocksLowerTriangular" | custom-call | tf_op jit(solution)/shard_map/jit(_solve_triangular)/triangular_solve | solution.py:58
  663.1 4.5 fusion
  667.5 4.5 reshape.76
  (66 shorter events, 26.9 us)
Async XLA Ops:
  6.5 16.6 %copy-start = (f32[4,2,5]{2,1,0:T(2,128)S(1)}, f32[4,2,5]{2,1,0:T(2,128)}, u32[]{:S(2)}) copy-start(f32[4,2,5]{2,1,0:T(2,128)} %param.7) | copy-start | bytes 484
  6.5 198.8 %all-reduce.5.cloned.1.call-start = ((), (), s32[]{:S(2)}) async-start(), calls=%async_computation | async-start | bytes 262144 | tf_op jit(solution)/shard_map/psum | solution.py:95
  6.6 11.0 %slice-start = ((s8[8388608]{0:T(1024)(128)(4,1)}), s8[4194304]{0:T(1024)(128)(4,1)S(1)}, s32[]{:S(2)}) async-start(s8[8388608]{0:T(1024)(128)(4,1)} %bitcast.115), calls=%async_computation.4 | async-start | bytes 8388608
  8.5 9.1 %slice-start.1 = ((s8[8388608]{0:T(1024)(128)(4,1)}), s8[4194304]{0:T(1024)(128)(4,1)S(1)}, s32[]{:S(2)}) async-start(s8[8388608]{0:T(1024)(128)(4,1)} %bitcast.115), calls=%async_computation.5 | async-start | bytes 8388608
  34.6 46.8 %collective-permute-start = (bf16[128,8192]{0,1:T(8,128)(2,1)}, bf16[128,8192]{0,1:T(8,128)(2,1)}, u32[]{:S(2)}, u32[]{:S(2)}) collective-permute-start(bf16[128,8192]{0,1:T(8,128)(2,1)} %bitcast.114), channel_id=1, source_target_pairs={{0,16},{16,0},{32,48},{48,32},{64,80},{80,64},{96,112},{112,96},{1... | collective-permute-start | bytes 6291464 | tf_op jit(solution)/shard_map/ppermute | solution.py:16
  83.9 4.7 copy-start.2
  90.6 258.6 %all-reduce.7.cloned.1.call-start = ((), (), s32[]{:S(2)}) async-start(), calls=%async_computation.1 | async-start | bytes 262144 | tf_op jit(solution)/shard_map/psum | solution.py:95
  230.9 3.3 copy-start.3
  239.1 254.2 %all-reduce.9.cloned.1.call-start = ((), (), s32[]{:S(2)}) async-start(), calls=%async_computation.2 | async-start | bytes 262144 | tf_op jit(solution)/shard_map/psum | solution.py:95
  374.7 3.3 copy-start.4
  382.9 254.4 %all-reduce.11.cloned.1.call-start = ((), (), s32[]{:S(2)}) async-start(), calls=%async_computation.3 | async-start | bytes 262144 | tf_op jit(solution)/shard_map/psum | solution.py:95
  518.8 3.2 copy-start.5
  663.1 8.9 %copy-start.1 = (f32[4,2,5]{2,1,0:T(2,128)S(1)}, f32[4,2,5]{2,1,0:T(2,128)}, u32[]{:S(2)}) copy-start(f32[4,2,5]{2,1,0:T(2,128)} %param.7) | copy-start | bytes 484
Sparse Core Ops, SparseCore 0:
  90.7 114.6 all-reduce.4
  239.2 110.0 all-reduce.6
  383.0 110.2 all-reduce.8
  527.1 110.2 all-reduce.10
where the time goes:
time: 686 us; the launch traced here: 679 us
  waiting for transfers between devices  482 us (70%)
  other arithmetic  93.9 us (14%)
  matrix products  71 us (10%)
  between operations  13.9 us (2%)
  starting transfers between devices  10.9 us (2%)
  local copies, waits for them, and re-layouts  7.53 us (1%)
    psum x4, waiting for transfers between devices, local(): image_cols = lax.psum(image_cols, 'space')  437 us
    another operation x12, other arithmetic, orthonormal(): factor = jnp.linalg.cholesky(product)  49.8 us
    ppermute x1, waiting for transfers between devices, from_partner(): return lax.ppermute(value, axis, pairs)  44.5 us
    another operation x8, other arithmetic, orthonormal(): return jax.scipy.linalg.solve_triangular(factor, image_cols.T, lower=True).T  41.5 us
  transfers between devices with their start and end apart: 5, of which 5 were waited for; matrix products, arithmetic and copies ran while one was open for 0% of the time, Pallas kernels for 0%

commit v1 on v0

v1 whole, which is shorter than its diff:
```python
import functools
import math

import jax
import jax.numpy as jnp
from jax import lax
from jax.experimental import pallas as pl
from jax.experimental.pallas import tpu as pltpu
from jax.sharding import PartitionSpec as P

SNAP = 128
RANK = 128
VARS = 4
ITERS = 4
ROWS = 8
FINE_ROWS = 16
FINE = 256
CELLS = 1024
TAPS = 5
SPACE = 16

f32 = jnp.float32
bf16 = jnp.bfloat16
HIGHEST = lax.Precision.HIGHEST
MESH = pl.DeviceIdType.MESH


def dot(a, b, ca, cb, precision=None):
    return lax.dot_general(
        a, b, (((ca,), (cb,)), ((), ())), preferred_element_type=f32, precision=precision
    )


def lon_weights(taps, v, level):
    fine = lax.broadcasted_iota(jnp.int32, (FINE, FINE // 2), 0)
    coarse = lax.broadcasted_iota(jnp.int32, (FINE, FINE // 2), 1)
    offset = fine - 2 * coarse + TAPS // 2
    weights = jnp.zeros((FINE, FINE // 2), f32)
    for u in range(TAPS):
        weights = jnp.where(offset == u, taps[v, level, u], weights)
    high = weights.astype(bf16)
    low = (weights - high.astype(f32)).astype(bf16)
    return jnp.concatenate([high, low], axis=1)


def coarsen_block(fine, across, lat, lon, v, level, put):
    weights = lon_weights(lon, v, level)
    both = jnp.dot(
        fine[...].reshape(SNAP * FINE_ROWS, FINE), weights, preferred_element_type=f32
    )
    across[...] = both[:, : FINE // 2] + both[:, FINE // 2 :]
    rows = [across[pl.ds(k, SNAP, stride=FINE_ROWS), :] for k in range(FINE_ROWS)]
    for i in range(ROWS):
        total = None
        for a in range(TAPS):
            k = 2 * i + a - TAPS // 2
            if 0 <= k < FINE_ROWS:
                term = rows[k] * lat[v, level, a]
                total = term if total is None else total + term
        put(i, total.astype(bf16))


def wait_bytes(ref, sem):
    pltpu.make_async_copy(ref, ref, sem).wait()


def gram_kernel(
    x_hbm, lat, lon,
    kept, got, snd, gram,
    fine, across, own_src, own_rcv, own_all, cross_src, cross_rcv, cross_all,
    load_sem, chunk_send, chunk_recv, send_sem, recv_sem,
):
    tm = lax.axis_index("tm")
    sp = lax.axis_index("space")
    e = lax.rem(tm, 2)
    f = 1 - e
    pt = tm + 1 - 2 * e

    loads = []
    for c in range(2 * VARS):
        level = f if c < VARS else e
        load = pltpu.make_async_copy(x_hbm.at[0, :, c % VARS, level], fine.at[c], load_sem.at[c])
        load.start()
        loads.append(load)

    barrier = pltpu.get_barrier_semaphore()

    def greet(i, carry):
        s = lax.rem(sp + 1 + i, SPACE)
        pl.semaphore_signal(barrier, inc=1, device_id=(tm, s), device_id_type=MESH)
        return carry

    lax.fori_loop(0, SPACE - 1, greet, 0)

    def greet_partner(i, carry):
        pl.semaphore_signal(barrier, inc=1, device_id=(pt, i), device_id_type=MESH)
        return carry

    lax.fori_loop(0, SPACE, greet_partner, 0)

    copies = []
    for v in range(VARS):
        loads[v].wait()

        def put(i, value, v=v):
            snd[v, :, 128 * i : 128 * i + 128] = value

        coarsen_block(fine.at[v], across.at[v % 2], lat, lon, v, f, put)
        if v == 0:
            pl.semaphore_wait(barrier, 2 * SPACE - 1)
        copy = pltpu.make_async_remote_copy(
            src_ref=snd.at[v],
            dst_ref=got.at[v],
            send_sem=chunk_send.at[v],
            recv_sem=chunk_recv.at[v],
            device_id=(pt, sp),
            device_id_type=MESH,
        )
        copy.start()
        copies.append(copy)
    for v in range(VARS):
        loads[VARS + v].wait()

        def put_own(i, value, v=v):
            kept[v, :, 128 * i : 128 * i + 128] = value

        coarsen_block(fine.at[VARS + v], across.at[v % 2], lat, lon, v, e, put_own)

    own = None
    for v in range(VARS):
        for block in (snd[v], kept[v]):
            term = dot(block, block, 1, 1)
            own = term if own is None else own + term
    for b in range(SPACE):
        own_src[b] = own[8 * b : 8 * b + 8, :]

    def far_first(i):
        half = lax.div(i + 1, 2)
        return lax.rem(sp + SPACE // 2 + (1 - 2 * lax.rem(i, 2)) * half, SPACE)

    def scatter_own(i, carry):
        s = far_first(i)
        pltpu.make_async_remote_copy(
            src_ref=own_src.at[s],
            dst_ref=own_rcv.at[sp],
            send_sem=send_sem.at[0],
            recv_sem=recv_sem.at[0],
            device_id=(tm, s),
            device_id_type=MESH,
        ).start()
        return carry

    lax.fori_loop(0, SPACE - 1, scatter_own, 0)
    own_rcv[sp] = own_src[sp]
    wait_bytes(own_rcv.at[pl.ds(0, SPACE - 1)], recv_sem.at[0])
    total = own_rcv[0]
    for s in range(1, SPACE):
        total = total + own_rcv[s]
    mine = e * SPACE + sp
    own_all[mine] = total

    def gather_to(src, sem, partner):
        def body(i, carry):
            s = far_first(i)
            pltpu.make_async_remote_copy(
                src_ref=src,
                dst_ref=src,
                send_sem=send_sem.at[sem],
                recv_sem=recv_sem.at[sem],
                device_id=(pt if partner else tm, s),
                device_id_type=MESH,
            ).start()
            return carry

        lax.fori_loop(0, SPACE if partner else SPACE - 1, body, 0)

    gather_to(own_all.at[mine], 1, True)
    gather_to(own_all.at[mine], 1, False)

    cross = None
    for v in range(VARS):
        copies[v].wait_recv()
        term = dot(kept[v], got[v], 1, 1)
        cross = term if cross is None else cross + term
    cross = jnp.where(e == 0, cross, cross.T)
    for b in range(2 * SPACE):
        cross_src[b] = cross[4 * b : 4 * b + 4, :]
    slot = 2 * sp + e

    def scatter_cross(partner):
        def body(i, carry):
            s = far_first(i)
            pltpu.make_async_remote_copy(
                src_ref=cross_src.at[2 * s + (f if partner else e)],
                dst_ref=cross_rcv.at[slot],
                send_sem=send_sem.at[2],
                recv_sem=recv_sem.at[2],
                device_id=(pt if partner else tm, s),
                device_id_type=MESH,
            ).start()
            return carry

        lax.fori_loop(0, SPACE if partner else SPACE - 1, body, 0)

    scatter_cross(True)
    scatter_cross(False)
    cross_rcv[slot] = cross_src[slot]
    wait_bytes(cross_rcv.at[pl.ds(0, 2 * SPACE - 1)], recv_sem.at[2])
    total = cross_rcv[0]
    for s in range(1, 2 * SPACE):
        total = total + cross_rcv[s]
    cross_all[slot] = total
    gather_to(cross_all.at[slot], 3, True)
    gather_to(cross_all.at[slot], 3, False)

    wait_bytes(own_all.at[pl.ds(0, 2 * SPACE - 1)], recv_sem.at[1])
    for b in range(SPACE):
        gram[8 * b : 8 * b + 8, :SNAP] = own_all[b]
        gram[SNAP + 8 * b : SNAP + 8 * b + 8, SNAP:] = own_all[SPACE + b]
    wait_bytes(cross_all.at[pl.ds(0, 2 * SPACE - 1)], recv_sem.at[3])
    for b in range(2 * SPACE):
        gram[4 * b : 4 * b + 4, SNAP:] = cross_all[b]
    gram[SNAP:, :SNAP] = gram[:SNAP, SNAP:].T

    for v in range(VARS):
        copies[v].wait_send()
    wait_bytes(own_src.at[pl.ds(0, SPACE - 1)], send_sem.at[0])
    wait_bytes(own_all.at[pl.ds(0, 2 * SPACE - 1)], send_sem.at[1])
    wait_bytes(cross_src.at[pl.ds(0, 2 * SPACE - 1)], send_sem.at[2])
    wait_bytes(cross_all.at[pl.ds(0, 2 * SPACE - 1)], send_sem.at[3])


def pair_gram(snapshots, lat, lon):
    vmem = pltpu.VMEM
    return pl.pallas_call(
        gram_kernel,
        out_shape=(
            jax.ShapeDtypeStruct((VARS, SNAP, CELLS), bf16),
            jax.ShapeDtypeStruct((VARS, SNAP, CELLS), bf16),
            jax.ShapeDtypeStruct((VARS, SNAP, CELLS), bf16),
            jax.ShapeDtypeStruct((2 * SNAP, 2 * SNAP), f32),
        ),
        in_specs=[
            pl.BlockSpec(memory_space=pl.ANY),
            pl.BlockSpec(memory_space=pltpu.SMEM),
            pl.BlockSpec(memory_space=pltpu.SMEM),
        ],
        out_specs=(pl.BlockSpec(memory_space=vmem),) * 4,
        scratch_shapes=[
            vmem((2 * VARS, SNAP, FINE_ROWS, FINE), bf16),
            vmem((2, SNAP * FINE_ROWS, FINE // 2), f32),
            vmem((SPACE, 8, SNAP), f32),
            vmem((SPACE, 8, SNAP), f32),
            vmem((2 * SPACE, 8, SNAP), f32),
            vmem((2 * SPACE, 4, SNAP), f32),
            vmem((2 * SPACE, 4, SNAP), f32),
            vmem((2 * SPACE, 4, SNAP), f32),
            pltpu.SemaphoreType.DMA((2 * VARS,)),
            pltpu.SemaphoreType.DMA((VARS,)),
            pltpu.SemaphoreType.DMA((VARS,)),
            pltpu.SemaphoreType.DMA((4,)),
            pltpu.SemaphoreType.DMA((4,)),
        ],
        compiler_params=pltpu.CompilerParams(collective_id=0, has_side_effects=True),
        name="pair_gram",
    )(snapshots, lat, lon)


def lanes(x, k):
    return jnp.broadcast_to(x[:, k : k + 1], (8, RANK))


def sublanes(x, r):
    return jnp.broadcast_to(x[r : r + 1, :], (8, RANK))


def inverse_factor(product, eye):
    a = [product[8 * i : 8 * i + 8, :] for i in range(RANK // 8)]
    w = [eye[8 * i : 8 * i + 8, :] for i in range(RANK // 8)]
    sub = lax.broadcasted_iota(jnp.int32, (8, RANK), 0)
    out = []
    for j in range(RANK // 8):
        cols = [lanes(a[j], 8 * j + b) for b in range(8)]
        d = {(p, q): sublanes(cols[q], p) for q in range(8) for p in range(q + 1)}
        inv = []
        m = {}
        for k in range(8):
            inv.append(1.0 / d[k, k])
            for q in range(k + 1, 8):
                m[k, q] = d[k, q] * inv[k]
            for q in range(k + 1, 8):
                for p in range(k + 1, q + 1):
                    d[p, q] = d[p, q] - d[k, p] * m[k, q]
        rows_a, rows_w = [], []
        for q in range(8):
            ra, rw = sublanes(a[j], q), sublanes(w[j], q)
            for p in range(q):
                ra = ra - m[p, q] * rows_a[p]
                rw = rw - m[p, q] * rows_w[p]
            rows_a.append(ra)
            rows_w.append(rw)
        block = rows_w[0] * lax.rsqrt(d[0, 0])
        for q in range(1, 8):
            block = jnp.where(sub == q, rows_w[q] * lax.rsqrt(d[q, q]), block)
        out.append(block)
        for i in range(j + 1, RANK // 8):
            c = [lanes(a[i], 8 * j + b) for b in range(8)]
            for q in range(8):
                for p in range(q):
                    c[q] = c[q] - m[p, q] * c[p]
            for q in range(8):
                factor = c[q] * inv[q]
                a[i] = a[i] - factor * rows_a[q]
                w[i] = w[i] - factor * rows_w[q]
    return jnp.concatenate(out, axis=0)


def iterate_kernel(gram, coef):
    row = lax.broadcasted_iota(jnp.int32, (RANK, RANK), 0)
    col = lax.broadcasted_iota(jnp.int32, (RANK, RANK), 1)
    eye = (row == col).astype(f32)

    def orthonormal(image):
        product = dot(image, image, 1, 1, HIGHEST)
        return dot(inverse_factor(product, eye), image, 1, 0, HIGHEST)

    basis = orthonormal(gram[:RANK, :] + gram[RANK:, :])
    basis = lax.fori_loop(
        0, ITERS - 1, lambda _, b: orthonormal(dot(b, gram[...], 1, 0, HIGHEST)), basis
    )
    coef[...] = basis.astype(bf16)


def iterate(gram):
    return pl.pallas_call(
        iterate_kernel,
        out_shape=jax.ShapeDtypeStruct((RANK, 2 * SNAP), bf16),
        in_specs=[pl.BlockSpec(memory_space=pltpu.VMEM)],
        out_specs=pl.BlockSpec(memory_space=pltpu.VMEM),
        cost_estimate=pl.CostEstimate(flops=20_000_000_000, bytes_accessed=400_000, transcendentals=0),
        name="iterate",
    )(gram)


def merge_kernel(coef, kept, got, snd, rcv, out):
    e = lax.rem(lax.axis_index("tm"), 2)
    low, high = coef[:, :SNAP], coef[:, SNAP:]
    lower = e == 0
    own = jnp.where(lower, low, high)
    other = jnp.where(lower, high, low)
    row = lax.broadcasted_iota(jnp.int32, (2 * RANK, RANK), 0)
    col = lax.broadcasted_iota(jnp.int32, (2 * RANK, RANK), 1)

    def spread(level, value):
        return dot((row == 2 * col + level).astype(bf16), value, 1, 0).astype(bf16)

    left = jnp.concatenate(
        [spread(e, own), spread(e, other), spread(1 - e, own), spread(1 - e, other)], axis=1
    )
    for v in range(VARS):
        right = jnp.concatenate([kept[v], got[v], snd[v], rcv[v]], axis=0)
        product = dot(left, right, 1, 0) * (1.0 / math.sqrt(2 * SNAP))
        out[:, v] = product.astype(bf16).reshape(RANK, 2, CELLS)


def merge(coef, kept, got, snd, rcv):
    return pl.pallas_call(
        merge_kernel,
        out_shape=jax.ShapeDtypeStruct((RANK, VARS, 2, CELLS), bf16),
        in_specs=[pl.BlockSpec(memory_space=pltpu.VMEM)] * 5,
        out_specs=pl.BlockSpec(memory_space=pltpu.VMEM),
        name="merge",
    )(coef, kept, got, snd, rcv)


def local(snapshots, lat_taps, lon_taps):
    kept, got, snd, gram = pair_gram(snapshots, lat_taps, lon_taps)
    pairs = [(source, source ^ 1) for source in range(lax.axis_size("tm"))]
    rcv = lax.ppermute(kept, "tm", pairs)
    coef = iterate(gram)
    return merge(coef, kept, got, snd, rcv)[None]


def solution(mesh):
    return jax.shard_map(
        local,
        mesh=mesh,
        in_specs=(
            P("tm", None, None, "space", None, None),
            P(None, "space", None),
            P(None, "space", None),
        ),
        out_specs=P("tm", None, None, "space", None),
        check_vma=False,
    )
```

time: 686 us -> 79.7 us (0.12); the launches traced: 679 us -> 79.5 us
  waiting for transfers between devices: 482 us -> 0.93 us
  other arithmetic: 93.9 us -> 0 us
  Pallas kernels: 0 us -> 76.7 us
  matrix products: 71 us -> 0 us
  between operations: 13.9 us -> 0.01 us
  starting transfers between devices: 10.9 us -> 0.92 us
    psum x4 -> x0, waiting for transfers between devices: 437 us -> none  [local(): image_cols = lax.psum(image_cols, 'space')]
    another operation x20 -> x0, other arithmetic: 91.3 us -> none  [the longest x12 49.8 us: orthonormal(): factor = jnp.linalg.cholesky(product)]
    pallas_call x0 -> x3, Pallas kernels: none -> 76.7 us  [the longest x1 48.7 us: pair_gram(): pl.pallas_call(gram_kernel, out_shape=(jax.ShapeDtypeStruct((VARS, SNAP,...]
    dot_general x26 -> x0, matrix products: 66.2 us -> none  [the longest x4 11.3 us: local(): lax.dot_general(basis_low, stacked, (((0,), (0,)), ((), ())), preferred_e...]
    ppermute x1, waiting for transfers between devices: 44.5 us -> 0.93 us  [local(): rcv = lax.ppermute(kept, 'tm', pairs)]
    psum x4 -> x0, starting transfers between devices: 8.52 us -> none  [local(): image_cols = lax.psum(image_cols, 'space')]
  transfers between devices with their start and end apart: 5 -> 1, of which waited for: 5 -> 1; matrix products, arithmetic and copies ran while one was open for 0% -> 0% of each run, Pallas kernels for 0% -> 29%
where the time goes in v1:
time: 79.7 us; the launch traced here: 79.5 us
  Pallas kernels  76.7 us (96%)
  local copies, waits for them, and re-layouts  0.97 us (1%)
  waiting for transfers between devices  0.93 us (1%)
  starting transfers between devices  0.92 us (1%)
    pallas_call x1, Pallas kernels, pair_gram(): pl.pallas_call(gram_kernel, out_shape=(jax.ShapeDtypeStruct((VARS, SNAP,...  48.7 us
    pallas_call x1, Pallas kernels, iterate(): pl.pallas_call(iterate_kernel, out_shape=jax.ShapeDtypeStruct((RANK, 2 *...  23 us
    pallas_call x1, Pallas kernels, merge(): pl.pallas_call(merge_kernel, out_shape=jax.ShapeDtypeStruct((RANK, VARS,...  5.03 us
  transfers between devices with their start and end apart: 1, of which 1 were waited for; matrix products, arithmetic and copies ran while one was open for 0% of the time, Pallas kernels for 29%

profile of v1, /device:TPU:1, one launch (start us, length us, event | category | flops | bytes accessed | tf_op | source)
XLA Modules:
  0.0 79.5 jit_solution(9803822068641583728)
XLA Ops:
  0.0 48.7 %pair_gram.1 = (bf16[4,128,1024]{2,1,0:T(8,128)(2,1)}, bf16[4,128,1024]{2,1,0:T(8,128)(2,1)}, bf16[4,128,1024]{2,1,0:T(8,128)(2,1)}, f32[256,256]{1,0:T(8,128)}) custom-call(bf16[1,128,4,2,16,256]{5,4,3,2,1,0:T(8,128)(2,1)} %x_hbm.1, f32[4,2,5]{2,1,0:T(2,128)} %lat.1, f32[4,2,5]{2,1,0:T(2,128)} %lon.1), custom_call_target="tpu_custom_call" | custom-call | tf_op jit(solution)/shard_map/pair_gram/pallas_call | solution.py:235
  48.7 0.9 %collective-permute-start = (bf16[4,128,1024]{2,1,0:T(8,128)(2,1)}, bf16[4,128,1024]{2,1,0:T(8,128)(2,1)S(1)}, u32[]{:S(2)}, u32[]{:S(2)}) collective-permute-start(bf16[4,128,1024]{2,1,0:T(8,128)(2,1)} %get-tuple-element.10.kept), channel_id=1, source_target_pairs={{0,16},{16,0},{32,48},{48,32},{64,80},{80,64},{96,112},{112,96},{1... | collective-permute-start | bytes 3145736 | tf_op jit(solution)/shard_map/ppermute | solution.py:379
  49.7 23.0 %iterate.1.coef = bf16[128,256]{1,0:T(8,128)(2,1)} custom-call(f32[256,256]{1,0:T(8,128)} %get-tuple-element.9.gram), custom_call_target="tpu_custom_call" | custom-call | flops 20000000000 | bytes 400000 | tf_op jit(solution)/shard_map/iterate/pallas_call | solution.py:335
  72.6 0.9 %collective-permute-done.rcv = bf16[4,128,1024]{2,1,0:T(8,128)(2,1)S(1)} collective-permute-done((bf16[4,128,1024]{2,1,0:T(8,128)(2,1)}, bf16[4,128,1024]{2,1,0:T(8,128)(2,1)S(1)}, u32[]{:S(2)}, u32[]{:S(2)}) %collective-permute-start) | collective-permute-done | bytes 1048608 | tf_op jit(solution)/shard_map/ppermute | solution.py:379
  73.5 0.0 copy-start
  73.5 1.0 %copy-done = bf16[4,128,1024]{2,1,0:T(8,128)(2,1)} copy-done((bf16[4,128,1024]{2,1,0:T(8,128)(2,1)}, bf16[4,128,1024]{2,1,0:T(8,128)(2,1)S(1)}, u32[]{:S(2)}) %copy-start) | copy-done | bytes 1048600
  74.5 5.0 %merge.1 = bf16[128,4,2,1024]{3,2,1,0:T(2,128)(2,1)} custom-call(bf16[128,256]{1,0:T(8,128)(2,1)} %iterate.1.coef, bf16[4,128,1024]{2,1,0:T(8,128)(2,1)} %get-tuple-element.10.kept, bf16[4,128,1024]{2,1,0:T(8,128)(2,1)} %get-tuple-element.11.got, bf16[4,128,1024]{2,1,0:T(8,128)(2,1)} %get-tuple-element.12.snd, bf16[4,128,1024]{2,1,0:T(8,128)(2,1)} %copy-done), custom_call_target="tpu_custom_call" | custom-call | tf_op jit(solution)/shard_map/merge/pallas_call | solution.py:367
Async XLA Ops:
  48.7 24.8 %collective-permute-start = (bf16[4,128,1024]{2,1,0:T(8,128)(2,1)}, bf16[4,128,1024]{2,1,0:T(8,128)(2,1)S(1)}, u32[]{:S(2)}, u32[]{:S(2)}) collective-permute-start(bf16[4,128,1024]{2,1,0:T(8,128)(2,1)} %get-tuple-element.10.kept), channel_id=1, source_target_pairs={{0,16},{16,0},{32,48},{48,32},{64,80},{80,64},{96,112},{112,96},{1... | collective-permute-start | bytes 3145736 | tf_op jit(solution)/shard_map/ppermute | solution.py:379
  73.5 1.0 %copy-start = (bf16[4,128,1024]{2,1,0:T(8,128)(2,1)}, bf16[4,128,1024]{2,1,0:T(8,128)(2,1)S(1)}, u32[]{:S(2)}) copy-start(bf16[4,128,1024]{2,1,0:T(8,128)(2,1)S(1)} %collective-permute-done.rcv) | copy-start | bytes 3145732

commit v2 on v1

--- a/solution.py
+++ b/solution.py
@@ -18,6 +18,8 @@
 CELLS = 1024
 TAPS = 5
 SPACE = 16
+EARLY = 1
+AHEAD = 3
 
 f32 = jnp.float32
 bf16 = jnp.bfloat16
@@ -65,10 +67,10 @@
 
 
 def gram_kernel(
-    x_hbm, lat, lon,
-    kept, got, snd, gram,
-    fine, across, own_src, own_rcv, own_all, cross_src, cross_rcv, cross_all,
-    load_sem, chunk_send, chunk_recv, send_sem, recv_sem,
+    x_hbm, lat_hbm, lon_hbm,
+    early, late, got, snd, rest, gram,
+    lat, lon, fine, across, own_src, own_rcv, own_all, cross_src, cross_rcv, cross_all,
+    tap_sem, load_sem, chunk_send, chunk_recv, early_send, early_recv, send_sem, recv_sem,
 ):
     tm = lax.axis_index("tm")
     sp = lax.axis_index("space")
@@ -76,6 +78,15 @@
     f = 1 - e
     pt = tm + 1 - 2 * e
 
+    def kept(v):
+        return early.at[v] if v < EARLY else late.at[v - EARLY]
+
+    taps = [
+        pltpu.make_async_copy(lat_hbm, lat, tap_sem.at[0]),
+        pltpu.make_async_copy(lon_hbm, lon, tap_sem.at[1]),
+    ]
+    for copy in taps:
+        copy.start()
     loads = []
     for c in range(2 * VARS):
         level = f if c < VARS else e
@@ -98,6 +109,8 @@
 
     lax.fori_loop(0, SPACE, greet_partner, 0)
 
+    for copy in taps:
+        copy.wait()
     copies = []
     for v in range(VARS):
         loads[v].wait()
@@ -122,13 +135,13 @@
         loads[VARS + v].wait()
 
         def put_own(i, value, v=v):
-            kept[v, :, 128 * i : 128 * i + 128] = value
+            kept(v)[:, 128 * i : 128 * i + 128] = value
 
         coarsen_block(fine.at[VARS + v], across.at[v % 2], lat, lon, v, e, put_own)
 
     own = None
     for v in range(VARS):
-        for block in (snd[v], kept[v]):
+        for block in (snd[v], kept(v)[...]):
             term = dot(block, block, 1, 1)
             own = term if own is None else own + term
     for b in range(SPACE):
@@ -180,7 +193,7 @@
     cross = None
     for v in range(VARS):
         copies[v].wait_recv()
-        term = dot(kept[v], got[v], 1, 1)
+        term = dot(kept(v)[...], got[v], 1, 1)
         cross = term if cross is None else cross + term
     cross = jnp.where(e == 0, cross, cross.T)
     for b in range(2 * SPACE):
@@ -204,6 +217,17 @@
 
     scatter_cross(True)
     scatter_cross(False)
+    for v in range(EARLY):
+        copy = pltpu.make_async_remote_copy(
+            src_ref=early.at[v],
+            dst_ref=rest.at[v],
+            send_sem=early_send.at[v],
+            recv_sem=early_recv.at[v],
+            device_id=(pt, sp),
+            device_id_type=MESH,
+        )
+        copy.start()
+        copies.append(copy)
     cross_rcv[slot] = cross_src[slot]
     wait_bytes(cross_rcv.at[pl.ds(0, 2 * SPACE - 1)], recv_sem.at[2])
     total = cross_rcv[0]
@@ -222,8 +246,10 @@
         gram[4 * b : 4 * b + 4, SNAP:] = cross_all[b]
     gram[SNAP:, :SNAP] = gram[:SNAP, SNAP:].T
 
-    for v in range(VARS):
-        copies[v].wait_send()
+    for copy in copies:
+        copy.wait_send()
+    for copy in copies[VARS:]:
+        copy.wait_recv()
     wait_bytes(own_src.at[pl.ds(0, SPACE - 1)], send_sem.at[0])
     wait_bytes(own_all.at[pl.ds(0, 2 * SPACE - 1)], send_sem.at[1])
     wait_bytes(cross_src.at[pl.ds(0, 2 * SPACE - 1)], send_sem.at[2])
@@ -235,18 +261,22 @@
     return pl.pallas_call(
         gram_kernel,
         out_shape=(
+            jax.ShapeDtypeStruct((EARLY, SNAP, CELLS), bf16),
+            jax.ShapeDtypeStruct((VARS - EARLY, SNAP, CELLS), bf16),
             jax.ShapeDtypeStruct((VARS, SNAP, CELLS), bf16),
             jax.ShapeDtypeStruct((VARS, SNAP, CELLS), bf16),
-            jax.ShapeDtypeStruct((VARS, SNAP, CELLS), bf16),
+            jax.ShapeDtypeStruct((EARLY, SNAP, CELLS), bf16),
             jax.ShapeDtypeStruct((2 * SNAP, 2 * SNAP), f32),
         ),
         in_specs=[
-            pl.BlockSpec(memory_space=pl.ANY),
-            pl.BlockSpec(memory_space=pltpu.SMEM),
-            pl.BlockSpec(memory_space=pltpu.SMEM),
+            pl.BlockSpec(memory_space=pltpu.HBM),
+            pl.BlockSpec(memory_space=pltpu.HBM),
+            pl.BlockSpec(memory_space=pltpu.HBM),
         ],
-        out_specs=(pl.BlockSpec(memory_space=vmem),) * 4,
+        out_specs=(pl.BlockSpec(memory_space=vmem),) * 6,
         scratch_shapes=[
+            pltpu.SMEM((VARS, 2, TAPS), f32),
+            pltpu.SMEM((VARS, 2, TAPS), f32),
             vmem((2 * VARS, SNAP, FINE_ROWS, FINE), bf16),
             vmem((2, SNAP * FINE_ROWS, FINE // 2), f32),
             vmem((SPACE, 8, SNAP), f32),
@@ -255,13 +285,16 @@
             vmem((2 * SPACE, 4, SNAP), f32),
             vmem((2 * SPACE, 4, SNAP), f32),
             vmem((2 * SPACE, 4, SNAP), f32),
+            pltpu.SemaphoreType.DMA((2,)),
             pltpu.SemaphoreType.DMA((2 * VARS,)),
             pltpu.SemaphoreType.DMA((VARS,)),
             pltpu.SemaphoreType.DMA((VARS,)),
+            pltpu.SemaphoreType.DMA((EARLY,)),
+            pltpu.SemaphoreType.DMA((EARLY,)),
             pltpu.SemaphoreType.DMA((4,)),
             pltpu.SemaphoreType.DMA((4,)),
         ],
-        compiler_params=pltpu.CompilerParams(collective_id=0, has_side_effects=True),
+        compiler_params=pltpu.CompilerParams(collective_id=0, has_side_effects=True, vmem_limit_bytes=48 << 20),
         name="pair_gram",
     )(snapshots, lat, lon)
 
@@ -274,14 +307,31 @@
     return jnp.broadcast_to(x[r : r + 1, :], (8, RANK))
 
 
+def split3(x):
+    high = x.astype(bf16)
+    left = x - high.astype(f32)
+    middle = left.astype(bf16)
+    return high, middle, (left - middle.astype(f32)).astype(bf16)
+
+
+def tree_sum(terms):
+    while len(terms) > 1:
+        terms = [x + y for x, y in zip(terms[::2], terms[1::2])]
+    return terms[0]
+
+
 def inverse_factor(product, eye):
-    a = [product[8 * i : 8 * i + 8, :] for i in range(RANK // 8)]
-    w = [eye[8 * i : 8 * i + 8, :] for i in range(RANK // 8)]
+    blocks = RANK // 8
+    a = [product[8 * i : 8 * i + 8, :] for i in range(blocks)]
+    w = [eye[8 * i : 8 * i + 8, :] for i in range(blocks)]
     sub = lax.broadcasted_iota(jnp.int32, (8, RANK), 0)
     out = []
-    for j in range(RANK // 8):
+    for j in range(blocks):
+        last = j == blocks - 1
         cols = [lanes(a[j], 8 * j + b) for b in range(8)]
         d = {(p, q): sublanes(cols[q], p) for q in range(8) for p in range(q + 1)}
+        rows_a = [sublanes(a[j], q) for q in range(8)]
+        rows_w = [sublanes(w[j], q) for q in range(8)]
         inv = []
         m = {}
         for k in range(8):
@@ -291,27 +341,46 @@
             for q in range(k + 1, 8):
                 for p in range(k + 1, q + 1):
                     d[p, q] = d[p, q] - d[k, p] * m[k, q]
-        rows_a, rows_w = [], []
-        for q in range(8):
-            ra, rw = sublanes(a[j], q), sublanes(w[j], q)
-            for p in range(q):
-                ra = ra - m[p, q] * rows_a[p]
-                rw = rw - m[p, q] * rows_w[p]
-            rows_a.append(ra)
-            rows_w.append(rw)
-        block = rows_w[0] * lax.rsqrt(d[0, 0])
-        for q in range(1, 8):
-            block = jnp.where(sub == q, rows_w[q] * lax.rsqrt(d[q, q]), block)
-        out.append(block)
-        for i in range(j + 1, RANK // 8):
-            c = [lanes(a[i], 8 * j + b) for b in range(8)]
+                if not last:
+                    rows_a[q] = rows_a[q] - m[k, q] * rows_a[k]
+                rows_w[q] = rows_w[q] - m[k, q] * rows_w[k]
+        root = [lax.rsqrt(d[q, q]) for q in range(8)]
+
+        def pick(rows):
+            block = rows[0] * root[0]
+            for q in range(1, 8):
+                block = jnp.where(sub == q, rows[q] * root[q], block)
+            return block
+
+        block_w = pick(rows_w)
+        out.append(block_w)
+        if last:
+            break
+        far = j + AHEAD + 1
+        if far < blocks:
+            ah, am, al = split3(pick(rows_a))
+            wh, wm, wl = split3(block_w)
+            right = jnp.concatenate(
+                [
+                    jnp.concatenate(pair, axis=1)
+                    for pair in ((ah, wh), (am, wm), (ah, wh), (am, wm), (al, wl), (ah, wh))
+                ],
+                axis=0,
+            )
+            left = jnp.concatenate([ah, ah, am, am, ah, al], axis=0)[:, 8 * far :]
+            update = dot(left, right, 0, 0)
+        for i in range(j + 1, min(far, blocks)):
+            c = [lanes(a[i], 8 * j + q) for q in range(8)]
             for q in range(8):
                 for p in range(q):
                     c[q] = c[q] - m[p, q] * c[p]
-            for q in range(8):
-                factor = c[q] * inv[q]
-                a[i] = a[i] - factor * rows_a[q]
-                w[i] = w[i] - factor * rows_w[q]
+            factor = [c[q] * inv[q] for q in range(8)]
+            a[i] = a[i] - tree_sum([factor[q] * rows_a[q] for q in range(8)])
+            w[i] = w[i] - tree_sum([factor[q] * rows_w[q] for q in range(8)])
+        for i in range(far, blocks):
+            r = 8 * (i - far)
+            a[i] = a[i] - update[r : r + 8, :RANK]
+            w[i] = w[i] - update[r : r + 8, RANK:]
     return jnp.concatenate(out, axis=0)
 
 
@@ -338,47 +407,66 @@
         in_specs=[pl.BlockSpec(memory_space=pltpu.VMEM)],
         out_specs=pl.BlockSpec(memory_space=pltpu.VMEM),
         cost_estimate=pl.CostEstimate(flops=20_000_000_000, bytes_accessed=400_000, transcendentals=0),
+        compiler_params=pltpu.CompilerParams(vmem_limit_bytes=8 << 20),
         name="iterate",
     )(gram)
 
 
-def merge_kernel(coef, kept, got, snd, rcv, out):
-    e = lax.rem(lax.axis_index("tm"), 2)
-    low, high = coef[:, :SNAP], coef[:, SNAP:]
-    lower = e == 0
-    own = jnp.where(lower, low, high)
-    other = jnp.where(lower, high, low)
-    row = lax.broadcasted_iota(jnp.int32, (2 * RANK, RANK), 0)
-    col = lax.broadcasted_iota(jnp.int32, (2 * RANK, RANK), 1)
-
-    def spread(level, value):
-        return dot((row == 2 * col + level).astype(bf16), value, 1, 0).astype(bf16)
-
-    left = jnp.concatenate(
-        [spread(e, own), spread(e, other), spread(1 - e, own), spread(1 - e, other)], axis=1
-    )
-    for v in range(VARS):
-        right = jnp.concatenate([kept[v], got[v], snd[v], rcv[v]], axis=0)
-        product = dot(left, right, 1, 0) * (1.0 / math.sqrt(2 * SNAP))
-        out[:, v] = product.astype(bf16).reshape(RANK, 2, CELLS)
-
-
-def merge(coef, kept, got, snd, rcv):
+def merge_kernel(coef, early, late, got, snd, rest, rcv, out, left):
+    v = pl.program_id(0)
+
+    @pl.when(v == 0)
+    def _():
+        e = lax.rem(lax.axis_index("tm"), 2)
+        low, high = coef[:, :SNAP], coef[:, SNAP:]
+        own = jnp.where(e == 0, low, high)
+        other = jnp.where(e == 0, high, low)
+        row = lax.broadcasted_iota(jnp.int32, (2 * RANK, RANK), 0)
+        col = lax.broadcasted_iota(jnp.int32, (2 * RANK, RANK), 1)
+        for k, (level, value) in enumerate(((e, own), (e, other), (1 - e, own), (1 - e, other))):
+            spread = dot((row == 2 * col + level).astype(bf16), value, 1, 0)
+            left[:, SNAP * k : SNAP * k + SNAP] = spread.astype(bf16)
+
+    def put(kept, received):
+        right = jnp.concatenate([kept[0], got[0], snd[0], received[0]], axis=0)
+        product = dot(left[...], right, 1, 0) * (1.0 / math.sqrt(2 * SNAP))
+        out[:, 0] = product.astype(bf16).reshape(RANK, 2, CELLS)
+
+    @pl.when(v < EARLY)
+    def _():
+        put(early, rest)
+
+    @pl.when(v >= EARLY)
+    def _():
+        put(late, rcv)
+
+
+def merge(coef, early, late, got, snd, rest, rcv):
+    first = pl.BlockSpec((1, SNAP, CELLS), lambda v: (jnp.minimum(v, EARLY - 1), 0, 0))
+    second = pl.BlockSpec((1, SNAP, CELLS), lambda v: (jnp.maximum(v - EARLY, 0), 0, 0))
+    every = pl.BlockSpec((1, SNAP, CELLS), lambda v: (v, 0, 0))
     return pl.pallas_call(
         merge_kernel,
+        grid=(VARS,),
         out_shape=jax.ShapeDtypeStruct((RANK, VARS, 2, CELLS), bf16),
-        in_specs=[pl.BlockSpec(memory_space=pltpu.VMEM)] * 5,
-        out_specs=pl.BlockSpec(memory_space=pltpu.VMEM),
+        in_specs=[
+            pl.BlockSpec((RANK, 2 * SNAP), lambda v: (0, 0)),
+            first, second, every, every, first, second,
+        ],
+        out_specs=pl.BlockSpec((RANK, 1, 2, CELLS), lambda v: (0, v, 0, 0)),
+        scratch_shapes=[pltpu.VMEM((2 * RANK, 4 * SNAP), bf16)],
+        compiler_params=pltpu.CompilerParams(vmem_limit_bytes=16 << 20),
         name="merge",
-    )(coef, kept, got, snd, rcv)
+    )(coef, early, late, got, snd, rest, rcv)
 
 
 def local(snapshots, lat_taps, lon_taps):
-    kept, got, snd, gram = pair_gram(snapshots, lat_taps, lon_taps)
+    lat_taps, lon_taps = (pltpu.with_memory_space_constraint(t, pltpu.HBM) for t in (lat_taps, lon_taps))
+    early, late, got, snd, rest, gram = pair_gram(snapshots, lat_taps, lon_taps)
     pairs = [(source, source ^ 1) for source in range(lax.axis_size("tm"))]
-    rcv = lax.ppermute(kept, "tm", pairs)
+    rcv = lax.ppermute(late, "tm", pairs)
     coef = iterate(gram)
-    return merge(coef, kept, got, snd, rcv)[None]
+    return merge(coef, early, late, got, snd, rest, rcv)[None]
 
 
 def solution(mesh):

time: 79.7 us -> 68.4 us (0.86)
  Pallas kernels: 76.7 us -> 66.6 us
  local copies, waits for them, and re-layouts: 0.97 us -> 0 us
    pallas_call x1, Pallas kernels: 23 us -> 17.3 us  [iterate(): pl.pallas_call(iterate_kernel, out_shape=jax.ShapeDtypeStruct((RANK, 2 *...]
    pallas_call x2, Pallas kernels: 53.8 us -> 49.4 us  [the longest x1 46.2 us: pair_gram(): pl.pallas_call(gram_kernel, out_shape=(jax.ShapeDtypeStruct((EARLY, SNAP,...]
    unnamed x2 -> x0, local copies, waits for them, and re-layouts: 0.97 us -> none
  transfers between devices with their start and end apart: 1 -> 1, of which waited for: 1 -> 1; matrix products, arithmetic and copies ran while one was open for 0% -> 0% of each run, Pallas kernels for 29% -> 25%
where the time goes in v2:
time: 68.4 us
  Pallas kernels  66.6 us (97%)
  starting transfers between devices  0.93 us (1%)
  waiting for transfers between devices  0.78 us (1%)
    pallas_call x1, Pallas kernels, pair_gram(): pl.pallas_call(gram_kernel, out_shape=(jax.ShapeDtypeStruct((EARLY, SNAP,...  46.2 us
    pallas_call x1, Pallas kernels, iterate(): pl.pallas_call(iterate_kernel, out_shape=jax.ShapeDtypeStruct((RANK, 2 *...  17.3 us
    pallas_call x1, Pallas kernels, merge(): pl.pallas_call(merge_kernel, grid=(VARS,), out_shape=jax.ShapeDtypeStruct...  3.22 us
  transfers between devices with their start and end apart: 1, of which 1 were waited for; matrix products, arithmetic and copies ran while one was open for 0% of the time, Pallas kernels for 25%

profile of v2, /device:TPU:1, one launch (start us, length us, event | category | flops | bytes accessed | tf_op | source)
XLA Modules:
  0.0 68.4 jit_solution(383073300499221383)
XLA Ops:
  0.0 46.2 %pair_gram.1 = (bf16[1,128,1024]{2,1,0:T(8,128)(2,1)S(1)}, bf16[3,128,1024]{2,1,0:T(8,128)(2,1)S(1)}, bf16[4,128,1024]{2,1,0:T(8,128)(2,1)S(1)}, bf16[4,128,1024...) custom-call(bf16[1,128,4,2,16,256]{5,4,3,2,1,0:T(8,128)(2,1)} %x_hbm.1, ...), custom_call_target="tpu_custom_call" | custom-call | tf_op jit(solution)/shard_map/pair_gram/pallas_call | solution.py:261
  46.2 0.9 %collective-permute-start = (bf16[3,128,1024]{2,1,0:T(8,128)(2,1)S(1)}, bf16[3,128,1024]{2,1,0:T(8,128)(2,1)S(1)}, u32[]{:S(2)}, u32[]{:S(2)}) collective-permute-start(bf16[3,128,1024]{2,1,0:T(8,128)(2,1)S(1)} %get-tuple-element.13.late), channel_id=1, source_target_pairs={{0,16},{16,0},{32,48},{48,32},{64,80},{80,64},{96,112},{112,96},{1... | collective-permute-start | bytes 2359304 | tf_op jit(solution)/shard_map/ppermute | solution.py:467
  47.1 17.3 %iterate.1.coef = bf16[128,256]{1,0:T(8,128)(2,1)S(1)} custom-call(f32[256,256]{1,0:T(8,128)S(1)} %get-tuple-element.11.gram), custom_call_target="tpu_custom_call" | custom-call | flops 20000000000 | bytes 400000 | tf_op jit(solution)/shard_map/iterate/pallas_call | solution.py:404
  64.4 0.8 %collective-permute-done.rcv = bf16[3,128,1024]{2,1,0:T(8,128)(2,1)S(1)} collective-permute-done((bf16[3,128,1024]{2,1,0:T(8,128)(2,1)S(1)}, bf16[3,128,1024]{2,1,0:T(8,128)(2,1)S(1)}, u32[]{:S(2)}, u32[]{:S(2)}) %collective-permute-start) | collective-permute-done | bytes 786464 | tf_op jit(solution)/shard_map/ppermute | solution.py:467
  65.2 3.2 %merge.1 = bf16[128,4,2,1024]{3,2,1,0:T(2,128)(2,1)} custom-call(bf16[128,256]{1,0:T(8,128)(2,1)S(1)} %iterate.1.coef, bf16[1,128,1024]{2,1,0:T(8,128)(2,1)S(1)} %get-tuple-element.12.early, bf16[3,128,1024]{2,1,0:T(8,128)(2,1)S(1)} %get-tuple-element.13.late, bf16[4,128,1024]{2,1,0:T(8,128)(2,1)S(1)} %get-tuple-element.14.got, ...), custom_call_target="tpu_custom_call" | custom-call | tf_op jit(solution)/shard_map/merge/pallas_call | solution.py:448
Async XLA Ops:
  46.2 19.0 %collective-permute-start = (bf16[3,128,1024]{2,1,0:T(8,128)(2,1)S(1)}, bf16[3,128,1024]{2,1,0:T(8,128)(2,1)S(1)}, u32[]{:S(2)}, u32[]{:S(2)}) collective-permute-start(bf16[3,128,1024]{2,1,0:T(8,128)(2,1)S(1)} %get-tuple-element.13.late), channel_id=1, source_target_pairs={{0,16},{16,0},{32,48},{48,32},{64,80},{80,64},{96,112},{112,96},{1... | collective-permute-start | bytes 2359304 | tf_op jit(solution)/shard_map/ppermute | solution.py:467

commit v3 on v2

--- a/solution.py
+++ b/solution.py
@@ -18,7 +18,7 @@
 CELLS = 1024
 TAPS = 5
 SPACE = 16
-EARLY = 1
+HEAD = 40
 AHEAD = 3
 
 f32 = jnp.float32
@@ -70,7 +70,7 @@
     x_hbm, lat_hbm, lon_hbm,
     early, late, got, snd, rest, gram,
     lat, lon, fine, across, own_src, own_rcv, own_all, cross_src, cross_rcv, cross_all,
-    tap_sem, load_sem, chunk_send, chunk_recv, early_send, early_recv, send_sem, recv_sem,
+    tap_sem, load_sem, chunk_send, chunk_recv, early_send, early_recv, pair_sem, send_sem, recv_sem,
 ):
     tm = lax.axis_index("tm")
     sp = lax.axis_index("space")
@@ -79,7 +79,7 @@
     pt = tm + 1 - 2 * e
 
     def kept(v):
-        return early.at[v] if v < EARLY else late.at[v - EARLY]
+        return jnp.concatenate([early[v], late[v]], axis=0)
 
     taps = [
         pltpu.make_async_copy(lat_hbm, lat, tap_sem.at[0]),
@@ -91,36 +91,40 @@
     for c in range(2 * VARS):
         level = f if c < VARS else e
         load = pltpu.make_async_copy(x_hbm.at[0, :, c % VARS, level], fine.at[c], load_sem.at[c])
-        load.start()
         loads.append(load)
+    loads[0].start()
+    loads[1].start()
 
     barrier = pltpu.get_barrier_semaphore()
 
+    def far_first(i):
+        half = lax.div(i + 1, 2)
+        return lax.rem(sp + SPACE // 2 + (1 - 2 * lax.rem(i, 2)) * half, SPACE)
+
     def greet(i, carry):
-        s = lax.rem(sp + 1 + i, SPACE)
+        s = far_first(i)
         pl.semaphore_signal(barrier, inc=1, device_id=(tm, s), device_id_type=MESH)
         return carry
 
+    def greet_partner(i, carry):
+        s = far_first(i)
+        pl.semaphore_signal(barrier, inc=1, device_id=(pt, s), device_id_type=MESH)
+        return carry
+
+    lax.fori_loop(0, SPACE, greet_partner, 0)
     lax.fori_loop(0, SPACE - 1, greet, 0)
-
-    def greet_partner(i, carry):
-        pl.semaphore_signal(barrier, inc=1, device_id=(pt, i), device_id_type=MESH)
-        return carry
-
-    lax.fori_loop(0, SPACE, greet_partner, 0)
 
     for copy in taps:
         copy.wait()
     copies = []
     for v in range(VARS):
         loads[v].wait()
+        loads[v + 2].start()
 
         def put(i, value, v=v):
             snd[v, :, 128 * i : 128 * i + 128] = value
 
         coarsen_block(fine.at[v], across.at[v % 2], lat, lon, v, f, put)
-        if v == 0:
-            pl.semaphore_wait(barrier, 2 * SPACE - 1)
         copy = pltpu.make_async_remote_copy(
             src_ref=snd.at[v],
             dst_ref=got.at[v],
@@ -129,27 +133,30 @@
             device_id=(pt, sp),
             device_id_type=MESH,
         )
-        copy.start()
         copies.append(copy)
+        if v == 1:
+            pl.semaphore_wait(barrier, 2 * SPACE - 1)
+            copies[0].start()
+        if v >= 1:
+            copy.start()
     for v in range(VARS):
         loads[VARS + v].wait()
+        if v + 2 < VARS:
+            loads[VARS + v + 2].start()
 
         def put_own(i, value, v=v):
-            kept(v)[:, 128 * i : 128 * i + 128] = value
+            early[v, :, 128 * i : 128 * i + 128] = value[:HEAD]
+            late[v, :, 128 * i : 128 * i + 128] = value[HEAD:]
 
         coarsen_block(fine.at[VARS + v], across.at[v % 2], lat, lon, v, e, put_own)
 
     own = None
     for v in range(VARS):
-        for block in (snd[v], kept(v)[...]):
+        for block in (snd[v], kept(v)):
             term = dot(block, block, 1, 1)
             own = term if own is None else own + term
     for b in range(SPACE):
         own_src[b] = own[8 * b : 8 * b + 8, :]
-
-    def far_first(i):
-        half = lax.div(i + 1, 2)
-        return lax.rem(sp + SPACE // 2 + (1 - 2 * lax.rem(i, 2)) * half, SPACE)
 
     def scatter_own(i, carry):
         s = far_first(i)
@@ -187,13 +194,21 @@
 
         lax.fori_loop(0, SPACE if partner else SPACE - 1, body, 0)
 
-    gather_to(own_all.at[mine], 1, True)
+    pair_copy = pltpu.make_async_remote_copy(
+        src_ref=own_all.at[mine],
+        dst_ref=own_all.at[mine],
+        send_sem=pair_sem.at[0],
+        recv_sem=pair_sem.at[1],
+        device_id=(pt, sp),
+        device_id_type=MESH,
+    )
+    pair_copy.start()
     gather_to(own_all.at[mine], 1, False)
 
     cross = None
     for v in range(VARS):
         copies[v].wait_recv()
-        term = dot(kept(v)[...], got[v], 1, 1)
+        term = dot(kept(v), got[v], 1, 1)
         cross = term if cross is None else cross + term
     cross = jnp.where(e == 0, cross, cross.T)
     for b in range(2 * SPACE):
@@ -217,7 +232,7 @@
 
     scatter_cross(True)
     scatter_cross(False)
-    for v in range(EARLY):
+    for v in range(VARS):
         copy = pltpu.make_async_remote_copy(
             src_ref=early.at[v],
             dst_ref=rest.at[v],
@@ -226,8 +241,11 @@
             device_id=(pt, sp),
             device_id_type=MESH,
         )
+        copies.append(copy)
+    for copy in copies[VARS:-1]:
         copy.start()
-        copies.append(copy)
+    pair_copy.wait_recv()
+    gather_to(own_all.at[f * SPACE + sp], 1, False)
     cross_rcv[slot] = cross_src[slot]
     wait_bytes(cross_rcv.at[pl.ds(0, 2 * SPACE - 1)], recv_sem.at[2])
     total = cross_rcv[0]
@@ -236,8 +254,9 @@
     cross_all[slot] = total
     gather_to(cross_all.at[slot], 3, True)
     gather_to(cross_all.at[slot], 3, False)
-
-    wait_bytes(own_all.at[pl.ds(0, 2 * SPACE - 1)], recv_sem.at[1])
+    copies[-1].start()
+
+    wait_bytes(own_all.at[pl.ds(0, 2 * SPACE - 2)], recv_sem.at[1])
     for b in range(SPACE):
         gram[8 * b : 8 * b + 8, :SNAP] = own_all[b]
         gram[SNAP + 8 * b : SNAP + 8 * b + 8, SNAP:] = own_all[SPACE + b]
@@ -251,7 +270,8 @@
     for copy in copies[VARS:]:
         copy.wait_recv()
     wait_bytes(own_src.at[pl.ds(0, SPACE - 1)], send_sem.at[0])
-    wait_bytes(own_all.at[pl.ds(0, 2 * SPACE - 1)], send_sem.at[1])
+    wait_bytes(own_all.at[pl.ds(0, 2 * SPACE - 2)], send_sem.at[1])
+    pair_copy.wait_send()
     wait_bytes(cross_src.at[pl.ds(0, 2 * SPACE - 1)], send_sem.at[2])
     wait_bytes(cross_all.at[pl.ds(0, 2 * SPACE - 1)], send_sem.at[3])
 
@@ -261,11 +281,11 @@
     return pl.pallas_call(
         gram_kernel,
         out_shape=(
-            jax.ShapeDtypeStruct((EARLY, SNAP, CELLS), bf16),
-            jax.ShapeDtypeStruct((VARS - EARLY, SNAP, CELLS), bf16),
+            jax.ShapeDtypeStruct((VARS, HEAD, CELLS), bf16),
+            jax.ShapeDtypeStruct((VARS, SNAP - HEAD, CELLS), bf16),
             jax.ShapeDtypeStruct((VARS, SNAP, CELLS), bf16),
             jax.ShapeDtypeStruct((VARS, SNAP, CELLS), bf16),
-            jax.ShapeDtypeStruct((EARLY, SNAP, CELLS), bf16),
+            jax.ShapeDtypeStruct((VARS, HEAD, CELLS), bf16),
             jax.ShapeDtypeStruct((2 * SNAP, 2 * SNAP), f32),
         ),
         in_specs=[
@@ -289,8 +309,9 @@
             pltpu.SemaphoreType.DMA((2 * VARS,)),
             pltpu.SemaphoreType.DMA((VARS,)),
             pltpu.SemaphoreType.DMA((VARS,)),
-            pltpu.SemaphoreType.DMA((EARLY,)),
-            pltpu.SemaphoreType.DMA((EARLY,)),
+            pltpu.SemaphoreType.DMA((VARS,)),
+            pltpu.SemaphoreType.DMA((VARS,)),
+            pltpu.SemaphoreType.DMA((2,)),
             pltpu.SemaphoreType.DMA((4,)),
             pltpu.SemaphoreType.DMA((4,)),
         ],
@@ -384,18 +405,33 @@
     return jnp.concatenate(out, axis=0)
 
 
-def iterate_kernel(gram, coef):
+def spread_left(parts):
+    high, middle, low = parts
+    return jnp.concatenate([high, high, middle, middle, high, low], axis=1)
+
+
+def spread_right(parts):
+    high, middle, low = parts
+    return jnp.concatenate([high, middle, high, middle, low, high], axis=0)
+
+
+def iterate_kernel(gram, coef, gram_parts):
     row = lax.broadcasted_iota(jnp.int32, (RANK, RANK), 0)
     col = lax.broadcasted_iota(jnp.int32, (RANK, RANK), 1)
     eye = (row == col).astype(f32)
+    gram_parts[...] = spread_right(split3(gram[...]))
 
     def orthonormal(image):
         product = dot(image, image, 1, 1, HIGHEST)
-        return dot(inverse_factor(product, eye), image, 1, 0, HIGHEST)
+        inverse = inverse_factor(product, eye)
+        return dot(spread_left(split3(inverse)), spread_right(split3(image)), 1, 0)
 
     basis = orthonormal(gram[:RANK, :] + gram[RANK:, :])
     basis = lax.fori_loop(
-        0, ITERS - 1, lambda _, b: orthonormal(dot(b, gram[...], 1, 0, HIGHEST)), basis
+        0,
+        ITERS - 1,
+        lambda _, b: orthonormal(dot(spread_left(split3(b)), gram_parts[...], 1, 0)),
+        basis,
     )
     coef[...] = basis.astype(bf16)
 
@@ -407,6 +443,7 @@
         in_specs=[pl.BlockSpec(memory_space=pltpu.VMEM)],
         out_specs=pl.BlockSpec(memory_space=pltpu.VMEM),
         cost_estimate=pl.CostEstimate(flops=20_000_000_000, bytes_accessed=400_000, transcendentals=0),
+        scratch_shapes=[pltpu.VMEM((12 * SNAP, 2 * SNAP), bf16)],
         compiler_params=pltpu.CompilerParams(vmem_limit_bytes=8 << 20),
         name="iterate",
     )(gram)
@@ -427,23 +464,14 @@
             spread = dot((row == 2 * col + level).astype(bf16), value, 1, 0)
             left[:, SNAP * k : SNAP * k + SNAP] = spread.astype(bf16)
 
-    def put(kept, received):
-        right = jnp.concatenate([kept[0], got[0], snd[0], received[0]], axis=0)
-        product = dot(left[...], right, 1, 0) * (1.0 / math.sqrt(2 * SNAP))
-        out[:, 0] = product.astype(bf16).reshape(RANK, 2, CELLS)
-
-    @pl.when(v < EARLY)
-    def _():
-        put(early, rest)
-
-    @pl.when(v >= EARLY)
-    def _():
-        put(late, rcv)
+    right = jnp.concatenate([early[0], late[0], got[0], snd[0], rest[0], rcv[0]], axis=0)
+    product = dot(left[...], right, 1, 0) * (1.0 / math.sqrt(2 * SNAP))
+    out[:, 0] = product.astype(bf16).reshape(RANK, 2, CELLS)
 
 
 def merge(coef, early, late, got, snd, rest, rcv):
-    first = pl.BlockSpec((1, SNAP, CELLS), lambda v: (jnp.minimum(v, EARLY - 1), 0, 0))
-    second = pl.BlockSpec((1, SNAP, CELLS), lambda v: (jnp.maximum(v - EARLY, 0), 0, 0))
+    head = pl.BlockSpec((1, HEAD, CELLS), lambda v: (v, 0, 0))
+    tail = pl.BlockSpec((1, SNAP - HEAD, CELLS), lambda v: (v, 0, 0))
     every = pl.BlockSpec((1, SNAP, CELLS), lambda v: (v, 0, 0))
     return pl.pallas_call(
         merge_kernel,
@@ -451,7 +479,7 @@
         out_shape=jax.ShapeDtypeStruct((RANK, VARS, 2, CELLS), bf16),
         in_specs=[
             pl.BlockSpec((RANK, 2 * SNAP), lambda v: (0, 0)),
-            first, second, every, every, first, second,
+            head, tail, every, every, head, tail,
         ],
         out_specs=pl.BlockSpec((RANK, 1, 2, CELLS), lambda v: (0, v, 0, 0)),
         scratch_shapes=[pltpu.VMEM((2 * RANK, 4 * SNAP), bf16)],

time: 68.4 us -> 66.2 us (0.968)
  Pallas kernels: 66.6 us -> 65.2 us
  waiting for transfers between devices: 0.78 us -> 0.01 us
    pallas_call x1, Pallas kernels: 46.2 us -> 44.8 us  [pair_gram(): pl.pallas_call(gram_kernel, out_shape=(jax.ShapeDtypeStruct((VARS, HEAD,...]
    ppermute x1, waiting for transfers between devices: 0.78 us -> 0.01 us  [local(): rcv = lax.ppermute(late, 'tm', pairs)]
  transfers between devices with their start and end apart: 1 -> 1, of which waited for: 1 -> 0; matrix products, arithmetic and copies ran while one was open for 0% -> 0% of each run, Pallas kernels for 25% -> 26%
where the time goes in v3:
time: 66.2 us; the launch traced here: 66.1 us
  Pallas kernels  65.2 us (98%)
  starting transfers between devices  0.97 us (1%)
    pallas_call x1, Pallas kernels, pair_gram(): pl.pallas_call(gram_kernel, out_shape=(jax.ShapeDtypeStruct((VARS, HEAD,...  44.8 us
    pallas_call x1, Pallas kernels, iterate(): pl.pallas_call(iterate_kernel, out_shape=jax.ShapeDtypeStruct((RANK, 2 *...  17.1 us
    pallas_call x1, Pallas kernels, merge(): pl.pallas_call(merge_kernel, grid=(VARS,), out_shape=jax.ShapeDtypeStruct...  3.25 us
  transfers between devices with their start and end apart: 1, of which 0 were waited for; matrix products, arithmetic and copies ran while one was open for 0% of the time, Pallas kernels for 26%

profile of v3, /device:TPU:1, one launch (start us, length us, event | category | flops | bytes accessed | tf_op | source)
XLA Modules:
  0.0 66.1 jit_solution(7731107608844767789)
XLA Ops:
  0.0 44.8 %pair_gram.1 = (bf16[4,40,1024]{2,1,0:T(8,128)(2,1)S(1)}, bf16[4,88,1024]{2,1,0:T(8,128)(2,1)S(1)}, bf16[4,128,1024]{2,1,0:T(8,128)(2,1)S(1)}, bf16[4,128,1024]{...) custom-call(bf16[1,128,4,2,16,256]{5,4,3,2,1,0:T(8,128)(2,1)} %x_hbm.1, ...), custom_call_target="tpu_custom_call" | custom-call | tf_op jit(solution)/shard_map/pair_gram/pallas_call | solution.py:281
  44.9 1.0 %collective-permute-start = (bf16[4,88,1024]{2,1,0:T(8,128)(2,1)S(1)}, bf16[4,88,1024]{2,1,0:T(8,128)(2,1)S(1)}, u32[]{:S(2)}, u32[]{:S(2)}) collective-permute-start(bf16[4,88,1024]{2,1,0:T(8,128)(2,1)S(1)} %get-tuple-element.13.late), channel_id=1, source_target_pairs={{0,16},{16,0},{32,48},{48,32},{64,80},{80,64},{96,112},{112,96},{1... | collective-permute-start | bytes 2162696 | tf_op jit(solution)/shard_map/ppermute | solution.py:495
  45.8 17.1 %iterate.1.coef = bf16[128,256]{1,0:T(8,128)(2,1)S(1)} custom-call(f32[256,256]{1,0:T(8,128)S(1)} %get-tuple-element.11.gram), custom_call_target="tpu_custom_call" | custom-call | flops 20000000000 | bytes 400000 | tf_op jit(solution)/shard_map/iterate/pallas_call | solution.py:440
  62.9 0.0 collective-permute-done.rcv
  62.9 3.3 %merge.1 = bf16[128,4,2,1024]{3,2,1,0:T(2,128)(2,1)} custom-call(bf16[128,256]{1,0:T(8,128)(2,1)S(1)} %iterate.1.coef, bf16[4,40,1024]{2,1,0:T(8,128)(2,1)S(1)} %get-tuple-element.12.early, bf16[4,88,1024]{2,1,0:T(8,128)(2,1)S(1)} %get-tuple-element.13.late, bf16[4,128,1024]{2,1,0:T(8,128)(2,1)S(1)} %get-tuple-element.14.got, ...), custom_call_target="tpu_custom_call" | custom-call | tf_op jit(solution)/shard_map/merge/pallas_call | solution.py:476
Async XLA Ops:
  44.9 18.0 %collective-permute-start = (bf16[4,88,1024]{2,1,0:T(8,128)(2,1)S(1)}, bf16[4,88,1024]{2,1,0:T(8,128)(2,1)S(1)}, u32[]{:S(2)}, u32[]{:S(2)}) collective-permute-start(bf16[4,88,1024]{2,1,0:T(8,128)(2,1)S(1)} %get-tuple-element.13.late), channel_id=1, source_target_pairs={{0,16},{16,0},{32,48},{48,32},{64,80},{80,64},{96,112},{112,96},{1... | collective-permute-start | bytes 2162696 | tf_op jit(solution)/shard_map/ppermute | solution.py:495
